TPU v7x, 256 devices: a whole 4x4x8 slice. The times are simulated.
256 devices in a mesh: seq: 16 (over z, core), head: 16 (over y, x).
Axes of the slice: x: 4, y: 4, z: 8, core: 2. Of those that a mesh axis runs over, the one named last changes fastest.
Arguments:
- queries: bfloat16 [6144, 16384], P('seq', 'head'), may hold values from -5 to 5
- keys: bfloat16 [6144, 1024], P('seq', 'head'), may hold values from -5 to 5
- values: bfloat16 [6144, 1024], P('seq', 'head'), may hold values from -6 to 6
- feat_q: bfloat16 [128, 128, 128], P('head'), may hold values from -0.5 to 0.5
- feat_k: bfloat16 [128, 128, 128], P('head'), may hold values from -0.5 to 0.5
Outputs:
- grad_feat_q: float32 [128, 128, 128], P('head')
- grad_feat_k: float32 [128, 128, 128], P('head')
All inputs are finite; a program needn't handle non-finite values.
Results may differ from a plain program's by a relative error of at most 0.02.
Values may be sent and summed in bfloat16 or wider, within the bound.
A program may use at most 128 MiB of HBM per device.

v0:
```python
import math
import jax
import jax.numpy as jnp
from jax import lax
from jax.sharding import PartitionSpec as P

HIGHEST_MODE = lax.Precision.HIGHEST
MASKED_SCORE = -1e30


def from_partner(block, axis, stride):
    count = lax.axis_size(axis)
    route = []
    for low in range(count):
        high = low | 1 << stride
        if high != low and high < count:
            route += [(low, high), (high, low)]
    return lax.ppermute(block, axis, route)


def in_one_piece(arrays, axis, dim, along):
    columns = [a.reshape(*a.shape[:along], -1) for a in arrays]
    both = jnp.concatenate(columns, axis=along)
    filled, at, done = (lax.all_gather(both, axis, axis=dim, tiled=True), 0, [])
    for a, column in zip(arrays, columns):
        piece = filled[..., at : at + column.shape[along]]
        done.append(piece.reshape(*piece.shape[:along], *a.shape[along:]))
        at += column.shape[along]
    return tuple(done)


def together(arrays, axis):
    vector, at, done = (jnp.concatenate([a.reshape(-1) for a in arrays]), 0, [])
    so_far = lax.psum(vector, axis)
    for a in arrays:
        done.append(so_far[at : at + a.size].reshape(a.shape))
        at += a.size
    return tuple(done)


def split_wide(entries):
    high = entries.astype(jnp.bfloat16)
    low = (entries - high.astype(jnp.float32)).astype(jnp.bfloat16)
    return (high, low)


def wide_left(form, wide, narrow):
    high, low = split_wide(wide)
    return jnp.einsum(form, high, narrow, preferred_element_type=jnp.float32) + jnp.einsum(
        form, low, narrow, preferred_element_type=jnp.float32
    )


def wide_right(form, narrow, wide):
    high, low = split_wide(wide)
    return jnp.einsum(form, narrow, high, preferred_element_type=jnp.float32) + jnp.einsum(
        form, narrow, low, preferred_element_type=jnp.float32
    )


def attend_block(
    running, query_half, query_pos, key_rows, value_rows, key_first, group_count, score_scale
):
    row_peak, row_total, summed = running
    half_rows = query_half.shape[0]
    key_count = key_rows.shape[0]
    head_dim = key_rows.shape[1] // group_count
    grouped = query_half.reshape(half_rows, group_count, -1, head_dim)
    key_heads = key_rows.reshape(key_count, group_count, head_dim)
    value_heads = value_rows.reshape(key_count, group_count, head_dim)
    scores = (
        jnp.einsum("rgjd,kgd->gjrk", grouped, key_heads, preferred_element_type=jnp.float32)
        * score_scale
    )
    scores = scores.reshape(row_peak.shape[0], half_rows, key_count)
    key_pos = key_first + jnp.arange(key_count, dtype=jnp.int32)
    allowed = (key_pos[None, :] <= query_pos[:, None])[None]
    new_peak = jnp.maximum(row_peak, jnp.max(jnp.where(allowed, scores, MASKED_SCORE), axis=-1))
    weights = jnp.exp(jnp.where(allowed, scores - new_peak[..., None], MASKED_SCORE))
    factor = jnp.exp(row_peak - new_peak)
    row_total = row_total * factor + jnp.sum(weights, axis=-1)
    rounded = weights.astype(jnp.bfloat16).reshape(group_count, -1, half_rows, key_count)
    mixture = jnp.einsum("gjrk,kgd->gjrd", rounded, value_heads, preferred_element_type=jnp.float32)
    summed = summed * factor[..., None] + mixture.reshape(summed.shape)
    return (new_peak, row_total, summed)


def body(queries, keys, values, feat_q, feat_k):
    row_count = queries.shape[0]
    heads_here = feat_q.shape[0]
    head_dim = feat_q.shape[1]
    seq_count = lax.axis_size("seq")
    seq_place = lax.axis_index("seq")
    head_place = lax.axis_index("head")
    key_value = jnp.stack((keys, values))
    partner = from_partner(key_value, "head", 0)
    upper_half = head_place // (1 << 0) % 2 == 1
    key_value = jnp.where(
        upper_half,
        jnp.concatenate((partner, key_value), axis=2),
        jnp.concatenate((key_value, partner), axis=2),
    )
    group_count = key_value.shape[2] // head_dim
    group_size = heads_here // group_count
    query_pos = seq_place * row_count + jnp.arange(row_count, dtype=jnp.int32)
    half_rows = row_count // 2
    query_halves = (queries[:half_rows], queries[half_rows:])
    pos_halves = (query_pos[:half_rows], query_pos[half_rows:])
    top_halves = (jnp.max(pos_halves[0]), jnp.max(pos_halves[1]))
    score_scale = head_dim ** (-0.5)
    start_half = (
        jnp.full((heads_here, half_rows), MASKED_SCORE, jnp.float32),
        jnp.zeros((heads_here, half_rows), jnp.float32),
        jnp.zeros((heads_here, half_rows, head_dim), jnp.float32),
    )
    shard_part = lax.all_gather(key_value, "seq", axis=1, tiled=True)
    part_rows = shard_part.shape[1]
    block_rows = math.gcd(part_rows, 512)

    def one_step(step_index, halves_state):
        offset = step_index * block_rows
        key_rows = lax.dynamic_slice_in_dim(shard_part[0], offset, block_rows, 0)
        value_rows = lax.dynamic_slice_in_dim(shard_part[1], offset, block_rows, 0)
        updated = []
        for half_index in range(2):

            def attend_half(current, half_index=half_index):
                return attend_block(
                    current,
                    query_halves[half_index],
                    pos_halves[half_index],
                    key_rows,
                    value_rows,
                    offset,
                    group_count,
                    score_scale,
                )

            def unchanged(current):
                return current

            updated.append(
                lax.cond(
                    top_halves[half_index] >= offset,
                    attend_half,
                    unchanged,
                    halves_state[half_index],
                )
            )
        return tuple(updated)

    finished = lax.fori_loop(0, part_rows // block_rows, one_step, (start_half, start_half))
    teacher_out = jnp.concatenate(
        [
            (finished[half_index][2] / finished[half_index][1][..., None]).astype(jnp.bfloat16)
            for half_index in range(2)
        ],
        axis=1,
    )
    key_local = key_value[0].reshape(row_count, group_count, head_dim)
    value_local = key_value[1].reshape(row_count, group_count, head_dim)
    query_local = queries.reshape(row_count, heads_here, head_dim)
    query_pre = jnp.einsum("rhd,hdf->hrf", query_local, feat_q, preferred_element_type=jnp.float32)
    key_pre = jnp.einsum(
        "rgd,gjdf->gjrf",
        key_local,
        feat_k.reshape(group_count, group_size, head_dim, -1),
        preferred_element_type=jnp.float32,
    ).reshape(heads_here, row_count, -1)
    feat_count = query_pre.shape[-1]
    query_feat = jax.nn.softplus(query_pre).astype(jnp.bfloat16)
    key_feat = jax.nn.softplus(key_pre).astype(jnp.bfloat16)
    block_state = jnp.einsum(
        "gjrf,rgd->gjfd",
        key_feat.reshape(group_count, group_size, row_count, -1),
        value_local,
        preferred_element_type=jnp.float32,
    ).reshape(heads_here, feat_count, head_dim)
    block_norm = jnp.sum(key_feat, axis=1, dtype=jnp.float32)
    zero_pair = (jnp.zeros_like(block_state), jnp.zeros_like(block_norm))
    take_shard_part = tuple(
        (
            part.astype(jnp.float32)
            for part in in_one_piece(
                (block_state[None].astype(jnp.bfloat16), block_norm[None].astype(jnp.bfloat16)),
                "seq",
                0,
                3,
            )
        )
    )
    part_count = take_shard_part[0].shape[0]
    chosen = jnp.arange(part_count, dtype=jnp.int32) < seq_place
    before_state = zero_pair[0] + jnp.sum(
        jnp.where(chosen[:, None, None, None], take_shard_part[0], 0.0), axis=0
    )
    before_norm = zero_pair[1] + jnp.sum(
        jnp.where(chosen[:, None, None], take_shard_part[1], 0.0), axis=0
    )
    causal = jnp.arange(row_count)[:, None] >= jnp.arange(row_count)[None, :]
    affinity = jnp.einsum("hrf,hsf->hrs", query_feat, key_feat, preferred_element_type=jnp.float32)
    masked = jnp.where(causal[None], affinity, 0.0)
    local_mix = jnp.einsum(
        "gjrs,sgd->gjrd",
        masked.astype(jnp.bfloat16).reshape(group_count, group_size, row_count, row_count),
        value_local,
        preferred_element_type=jnp.float32,
    ).reshape(heads_here, row_count, head_dim)
    numerator = wide_right("hrf,hfd->hrd", query_feat, before_state) + local_mix
    denominator = wide_right("hrf,hf->hr", query_feat, before_norm) + jnp.sum(masked, axis=-1)
    student = numerator / denominator[..., None]
    total_tokens = row_count * seq_count
    grad_out = 2.0 * (student - teacher_out.astype(jnp.float32)) / total_tokens
    grad_numer = grad_out / denominator[..., None]
    grad_denom = -jnp.sum(grad_out * student, axis=-1) / denominator
    back_state = wide_right("hrf,hrd->hfd", query_feat, grad_numer)
    back_norm = wide_right("hrf,hr->hf", query_feat, grad_denom)

    def take_upper(running, shard_part):
        part_count = shard_part[0].shape[0]
        chosen = jnp.arange(part_count, dtype=jnp.int32) > seq_place
        return (
            running[0]
            + jnp.sum(jnp.where(chosen[:, None, None, None], shard_part[0], 0.0), axis=0),
            running[1] + jnp.sum(jnp.where(chosen[:, None, None], shard_part[1], 0.0), axis=0),
        )

    after_state, after_norm = take_upper(
        zero_pair,
        (
            lax.all_gather(back_state[None].astype(jnp.bfloat16), "seq", axis=0, tiled=True).astype(
                jnp.float32
            ),
            lax.all_gather(back_norm[None].astype(jnp.bfloat16), "seq", axis=0, tiled=True).astype(
                jnp.float32
            ),
        ),
    )
    grad_aff = wide_left(
        "gjrd,sgd->gjrs",
        grad_numer.reshape(group_count, group_size, row_count, head_dim),
        value_local,
    ).reshape(heads_here, row_count, row_count)
    grad_aff = jnp.where(causal[None], grad_aff + grad_denom[..., None], 0.0)
    grad_qfeat = (
        jnp.einsum("hrd,hfd->hrf", grad_numer, before_state, precision=HIGHEST_MODE)
        + grad_denom[..., None] * before_norm[:, None, :]
        + wide_left("hrs,hsf->hrf", grad_aff, key_feat)
    )
    grad_kfeat = (
        wide_right(
            "sgd,gjfd->gjsf",
            value_local,
            after_state.reshape(group_count, group_size, feat_count, head_dim),
        ).reshape(heads_here, row_count, feat_count)
        + after_norm[:, None, :]
        + wide_left("hrs,hrf->hsf", grad_aff, query_feat)
    )
    grad_wq = wide_right("rhd,hrf->hdf", query_local, grad_qfeat * jax.nn.sigmoid(query_pre))
    grad_wk = wide_right(
        "rgd,gjrf->gjdf",
        key_local,
        (grad_kfeat * jax.nn.sigmoid(key_pre)).reshape(
            group_count, group_size, row_count, feat_count
        ),
    ).reshape(heads_here, head_dim, feat_count)
    return tuple(
        (
            part.astype(jnp.float32)
            for part in together(
                (grad_wq.astype(jnp.bfloat16), grad_wk.astype(jnp.bfloat16)), "seq"
            )
        )
    )


def solution(mesh):
    return jax.shard_map(
        body,
        mesh=mesh,
        in_specs=(
            P("seq", "head"),
            P("seq", "head"),
            P("seq", "head"),
            P("head", None, None),
            P("head", None, None),
        ),
        out_specs=(P("head", None, None), P("head", None, None)),
        check_vma=False,
    )
```

profile of v0, /device:TPU:1, one launch (start us, length us, event | category | flops | bytes accessed | tf_op | source)
XLA Modules:
  0.0 392.3 jit_solution(10411164082974506304)
XLA Ops:
  9.3 2.1 collective-permute-start
  11.4 3.4 collective-permute-done
  18.1 1.1 fusion.123
  21.4 2.2 select_reduce_fusion.1
  23.7 38.1 %all-gather.8.cloned.1.call-done = bf16[2,6144,128]{2,1,0:T(8,128)(2,1)} async-done(((bf16[2,384,128]{2,1,0:T(8,128)(2,1)}), bf16[2,6144,128]{2,1,0:T(8,128)(2,1)}) %all-gather.8.cloned.1.call-update) | async-done | bytes 3145744 | tf_op jit(solution)/shard_map/all_gather | solution.py:116
  62.8 56.6 %while.23 = (s32[]{:T(128)}, f32[8,192]{1,0:T(8,128)S(1)}, f32[8,192]{1,0:T(8,128)S(1)}, f32[8,192,128]{2,1,0:T(8,128)}, f32[8,192]{1,0:T(8,128)S(1)}, /*index=5...) while((s32[]{:T(128)}, f32[8,192]{1,0:T(8,128)S(1)}, ...), condition=%wide.region_15.16_spmd, body=%wide.region_6.15_spmd.sunk | while | flops 823598080 | bytes 37431328 | solution.py:152
  64.0 2.1 fusion.153
  66.2 4.4 %conditional.4 = ((f32[8,192]{1,0:T(8,128)S(1)}, f32[8,192]{1,0:T(8,128)S(1)}, f32[8,192,128]{2,1,0:T(8,128)})) conditional(s32[]{:T(128)} %convert_element_type.400, (f32[8,192]{1,0:T(8,128)S(1)}, f32[8,192]{1,0:T(8,128)S(1)}, f32[8,192,128]{2,1,0:T(8,128)}) %tuple.74, (s32[]{:T(128)}, s32[192]{0:T(256)S(1)}, bf16[192,1024]{1,0:T(8,128)(2,1)S(1)}, ...), branch_computations={%region_7.7_spmd, %region_8.10_spmd} | conditional | flops 411799040 | bytes 18453340 | solution.py:143
  67.1 1.1 fusion.3
  68.2 1.5 fusion.14
  70.6 3.5 conditional.5
  71.5 1.1 fusion.27
  72.6 1.5 fusion.38
  75.3 2.1 fusion.153
  77.4 4.4 %conditional.4 = ((f32[8,192]{1,0:T(8,128)S(1)}, f32[8,192]{1,0:T(8,128)S(1)}, f32[8,192,128]{2,1,0:T(8,128)})) conditional(s32[]{:T(128)} %convert_element_type.400, (f32[8,192]{1,0:T(8,128)S(1)}, f32[8,192]{1,0:T(8,128)S(1)}, f32[8,192,128]{2,1,0:T(8,128)}) %tuple.74, (s32[]{:T(128)}, s32[192]{0:T(256)S(1)}, bf16[192,1024]{1,0:T(8,128)(2,1)S(1)}, ...), branch_computations={%region_7.7_spmd, %region_8.10_spmd} | conditional | flops 411799040 | bytes 18453340 | solution.py:143
  78.4 1.1 fusion.3
  79.5 1.4 fusion.14
  81.9 3.5 conditional.5
  82.8 1.1 fusion.27
  83.9 1.5 fusion.38
  86.6 2.1 fusion.153
  90.0 2.2 fusion.153
  93.5 2.1 fusion.153
  96.9 2.1 fusion.153
  100.3 2.1 fusion.153
  103.7 2.1 fusion.153
  107.1 2.1 fusion.153
  110.5 2.1 fusion.153
  113.9 2.1 fusion.153
  117.3 2.1 fusion.153
  120.3 1.5 copy.125
  121.8 2.5 copy.124
  124.3 2.4 divide_convert_fusion
  126.7 4.6 %slice.72 = bf16[16,8,128,128]{2,1,3,0:T(8,128)(2,1)} slice(bf16[16,8,128,129]{2,1,3,0:T(8,128)(2,1)} %all-gather.6.cloned.1.call-done), slice={[0:16], [0:8], [0:128], [0:128]} | slice | bytes 8388608 | tf_op jit(solution)/shard_map/slice | solution.py:26
  131.2 6.7 %copy.186 = bf16[16,8,128,128]{3,2,1,0:T(8,128)(2,1)} copy(bf16[16,8,128,128]{2,1,3,0:T(8,128)(2,1)} %slice.72) | data formatting | bytes 8388608
  137.9 3.2 select_reduce_fusion
  144.2 1.1 multiply_reduce_fusion
  145.8 1.2 fusion.69
  147.3 2.8 fusion.128
  152.9 1.2 copy-done.2
  154.5 1.7 divide_multiply_fusion
  158.5 91.9 %all-gather.1 = bf16[128,128]{1,0:T(8,128)(2,1)S(1)} all-gather(bf16[8,128]{1,0:T(8,128)(2,1)S(1)} %add_convert_fusion), channel_id=3, replica_groups=mesh['seq'=16,'head'=16] {'seq'}, dimensions={0}, use_global_device_ids=true | all-gather | bytes 34816 | tf_op jit(solution)/shard_map/all_gather | solution.py:234
  250.5 4.7 %fusion.117 = f32[8,384,128]{2,1,0:T(8,128)S(1)} fusion(bf16[8,384,128]{2,1,0:T(8,128)(2,1)S(1)} %select_convert_fusion.2, f32[8,384,384]{1,2,0:T(8,128)} %copy-done.2), kind=kOutput, calls=%fused_computation.179 | convolution fusion | flops 306708480 | bytes 7077888 | tf_op jit(solution)/shard_map/hrs,hrf->hsf/dot_general | solution.py:49
  255.2 1.9 fusion.113
  257.2 7.9 %all-gather.10.cloned.1.call-done = bf16[128,128,128]{2,1,0:T(8,128)(2,1)} async-done(((bf16[8,128,128]{2,1,0:T(8,128)(2,1)}), bf16[128,128,128]{2,1,0:T(8,128)(2,1)}) %all-gather.10.cloned.1.call-update) | async-done | bytes 4194320 | tf_op jit(solution)/shard_map/all_gather | solution.py:231
  265.1 3.2 fusion.48
  269.9 2.1 fusion.55
  274.2 108.8 %all-reduce.2.cloned.1.call-done = bf16[262144]{0:T(1024)(128)(2,1)} async-done(((bf16[262144]{0:T(1024)(128)(2,1)}), bf16[262144]{0:T(1024)(128)(2,1)}) %all-reduce.2.cloned.1.call-update) | async-done | bytes 524304 | tf_op jit(solution)/shard_map/psum | solution.py:34
  (165 shorter events, 31.3 us)
Async XLA Ops:
  7.2 10.8 %copy-start = (bf16[8,128,128]{2,1,0:T(8,128)(2,1)S(1)}, bf16[8,128,128]{2,1,0:T(8,128)(2,1)}, u32[]{:S(2)}) copy-start(bf16[8,128,128]{2,1,0:T(8,128)(2,1)} %param.15) | copy-start | bytes 786436
  7.2 9.3 %copy-start.5 = (bf16[384,1024]{1,0:T(8,128)(2,1)S(1)}, bf16[384,1024]{1,0:T(8,128)(2,1)}, u32[]{:S(2)}) copy-start(bf16[384,1024]{1,0:T(8,128)(2,1)} %param.11) | copy-start | bytes 2359300
  7.2 54.6 %all-gather.8.cloned.1.call-start = ((), (), s32[]{:S(2)}) async-start(), calls=%async_computation.1 | async-start | bytes 3342336 | tf_op jit(solution)/shard_map/all_gather | solution.py:116
  8.2 8.3 %copy-start.18 = (bf16[8,128,128]{2,1,0:T(8,128)(2,1)S(1)}, bf16[8,128,128]{2,1,0:T(8,128)(2,1)}, u32[]{:S(2)}) copy-start(bf16[8,128,128]{2,1,0:T(8,128)(2,1)} %param.14) | copy-start | bytes 786436
  9.3 5.5 %collective-permute-start = (bf16[2,384,64]{2,1,0:T(8,128)(2,1)S(1)}, bf16[2,384,64]{2,1,0:T(8,128)(2,1)S(1)}, u32[]{:S(2)}, u32[]{:S(2)}) collective-permute-start(bf16[2,384,64]{2,1,0:T(8,128)(2,1)S(1)} %pad_maximum_fusion.3), channel_id=1, source_target_pairs={{0,1},{1,0},{2,3},{3,2},{4,5},{5,4},{6,7},{7,6},{8,9},{9,8},{10,11... | collective-permute-start | bytes 294920 | tf_op jit(solution)/shard_map/ppermute | solution.py:18
  15.7 111.0 %all-gather.6.cloned.1.call-start = ((), (), s32[]{:S(2)}) async-start(), calls=%async_computation | async-start | bytes 4491264 | tf_op jit(solution)/shard_map/all_gather | solution.py:24
  17.0 2.2 copy-start.3
  17.0 1.1 copy-start.8
  19.2 1.2 copy-start.14
  19.2 2.2 copy-start.9
  21.2 243.9 %all-gather.10.cloned.1.call-start = ((), (), s32[]{:S(2)}) async-start(), calls=%async_computation.3 | async-start | bytes 4456448 | tf_op jit(solution)/shard_map/all_gather | solution.py:231
  67.1 1.1 copy-start.12
  69.7 0.9 copy-start.13
  78.4 1.2 copy-start.12
  81.0 0.9 copy-start.13
  119.5 0.9 copy-start.11
  141.8 2.4 copy-start.19
  142.2 1.9 copy-start.16
  142.3 1.9 copy-start.17
  147.0 236.0 %all-reduce.2.cloned.1.call-start = ((), (), s32[]{:S(2)}) async-start(), calls=%async_computation.2 | async-start | bytes 1048576 | tf_op jit(solution)/shard_map/psum | solution.py:34
  150.8 1.1 copy-start.10
  152.0 2.1 copy-start.2
  152.0 2.5 copy-start.4
  154.5 1.7 copy-start.6
  156.2 99.0 %slice-start = ((s8[4718592]{0:T(1024)(128)(4,1)}), s8[524288]{0:T(1024)(128)(4,1)S(1)}, s32[]{:S(2)}) async-start(s8[4718592]{0:T(1024)(128)(4,1)} %bitcast.271), calls=%async_computation.4 | async-start | bytes 1048576
  158.2 97.0 %slice-start.1 = ((s8[4718592]{0:T(1024)(128)(4,1)}), s8[4194304]{0:T(1024)(128)(4,1)S(1)}, s32[]{:S(2)}) async-start(s8[4718592]{0:T(1024)(128)(4,1)} %bitcast.271), calls=%async_computation.5 | async-start | bytes 8388608
  268.5 1.4 copy-start.7
  272.4 1.0 copy-start.15
  274.2 111.6 %copy-start.1 = (bf16[8,128,128]{2,1,0:T(8,128)(2,1)S(1)}, bf16[8,128,128]{2,1,0:T(8,128)(2,1)}, u32[]{:S(2)}) copy-start(bf16[8,128,128]{2,1,0:T(8,128)(2,1)} %param.15) | copy-start | bytes 786436
Sparse Core Ops, SparseCore 0:
  15.8 45.9 all-gather.7
  63.7 40.6 all-gather.5
  147.1 117.8 all-gather.9
  274.3 108.6 all-reduce.1
where the time goes:
time: 394 us; the launch traced here: 392 us
  waiting for transfers between devices  158 us (40%)
  blocking collectives  91.9 us (23%)
  local copies, waits for them, and re-layouts  53.3 us (14%)
  matrix products  36.4 us (9%)
  other arithmetic  20.1 us (5%)
  loops' own time  15.4 us (4%)
  between operations  14.2 us (4%)
    psum x1, waiting for transfers between devices, together(): so_far = lax.psum(vector, axis)  109 us
    all_gather x1, blocking collectives, body(): lax.all_gather(back_norm[None].astype(jnp.bfloat16), 'seq', axis=0, tiled...  91.9 us
    all_gather x1, waiting for transfers between devices, body(): shard_part = lax.all_gather(key_value, 'seq', axis=1, tiled=True)  38.1 us
    slice x12, local copies, waits for them, and re-layouts, one_step(): value_rows = lax.dynamic_slice_in_dim(shard_part[1], offset, block_rows, 0)  25.2 us
    another operation x1, loops' own time, body(): lax.fori_loop(0, part_rows // block_rows, one_step, (start_half, start_ha...  14.8 us
    unnamed x45, local copies, waits for them, and re-layouts  13.5 us
  transfers between devices with their start and end apart: 5, of which 4 were waited for; matrix products, arithmetic and copies ran while one was open for 18% of the time, Pallas kernels for 0%

commit v1 on v0

--- a/solution.py
+++ b/solution.py
@@ -113,7 +113,21 @@
         jnp.zeros((heads_here, half_rows), jnp.float32),
         jnp.zeros((heads_here, half_rows, head_dim), jnp.float32),
     )
-    shard_part = lax.all_gather(key_value, "seq", axis=1, tiled=True)
+    ways, here, hop = (lax.axis_size("seq"), lax.axis_index("seq"), key_value.shape[1])
+    shape = [n * ways if d == 1 else n for d, n in enumerate(key_value.shape)]
+    full = lax.dynamic_update_slice_in_dim(
+        jnp.zeros(shape, key_value.dtype), key_value, here * hop, axis=1
+    )
+    going_up = going_down = key_value
+    for far in range(1, ways // 2 + 1):
+        going_up = lax.ppermute(going_up, "seq", [(d, (d + 1) % ways) for d in range(ways)])
+        full = lax.dynamic_update_slice_in_dim(full, going_up, (here - far) % ways * hop, axis=1)
+        if 2 * far < ways:
+            going_down = lax.ppermute(going_down, "seq", [(d, (d - 1) % ways) for d in range(ways)])
+            full = lax.dynamic_update_slice_in_dim(
+                full, going_down, (here + far) % ways * hop, axis=1
+            )
+    shard_part = full
     part_rows = shard_part.shape[1]
     block_rows = math.gcd(part_rows, 512)
 

time: 394 us -> 458 us (1.16)
  blocking collectives: 91.9 us -> 137 us
  starting transfers between devices: 2.68 us -> 46.7 us
  waiting for transfers between devices: 158 us -> 128 us
  local copies, waits for them, and re-layouts: 53.3 us -> 33.7 us
  matrix products: 36.4 us -> 51.1 us
  other arithmetic: 20.1 us -> 25.4 us
    all_gather x1, blocking collectives: 91.9 us -> 137 us  [body(): lax.all_gather(back_norm[None].astype(jnp.bfloat16), 'seq', axis=0, tiled...]
    ppermute x0 -> x15, starting transfers between devices: none -> 44.3 us  [the longest x7 41.7 us: body(): lax.ppermute(going_down, 'seq', [(d, (d - 1) % ways) for d in range(ways)])]
    all_gather x1 -> x0, waiting for transfers between devices: 38.1 us -> none  [body(): shard_part = lax.all_gather(key_value, 'seq', axis=1, tiled=True)]
    slice x12, local copies, waits for them, and re-layouts: 25.2 us -> 2.46 us  [one_step(): value_rows = lax.dynamic_slice_in_dim(shard_part[1], offset, block_rows, 0)]
    ppermute x0 -> x15, waiting for transfers between devices: none -> 12.6 us  [the longest x8 9.17 us: body(): lax.ppermute(going_up, 'seq', [(d, (d + 1) % ways) for d in range(ways)])]
    unnamed x45 -> x51, local copies, waits for them, and re-layouts: 13.5 us -> 12.1 us
  transfers between devices with their start and end apart: 5 -> 19, of which waited for: 4 -> 8; matrix products, arithmetic and copies ran while one was open for 18% -> 14% of each run, Pallas kernels for 0% -> 0%
where the time goes in v1:
time: 458 us; the launch traced here: 454 us
  blocking collectives  137 us (30%)
  waiting for transfers between devices  128 us (28%)
  matrix products  51.1 us (11%)
  starting transfers between devices  46.7 us (10%)
  local copies, waits for them, and re-layouts  33.7 us (7%)
  other arithmetic  25.4 us (6%)
  loops' own time  17.6 us (4%)
  between operations  14.5 us (3%)
    all_gather x1, blocking collectives, body(): lax.all_gather(back_norm[None].astype(jnp.bfloat16), 'seq', axis=0, tiled...  137 us
    psum x1, waiting for transfers between devices, together(): so_far = lax.psum(vector, axis)  109 us
    ppermute x7, starting transfers between devices, body(): lax.ppermute(going_down, 'seq', [(d, (d - 1) % ways) for d in range(ways)])  41.7 us
    another operation x1, loops' own time, body(): lax.fori_loop(0, part_rows // block_rows, one_step, (start_half, start_ha...  17 us
    unnamed x51, local copies, waits for them, and re-layouts  12.1 us
    ppermute x8, waiting for transfers between devices, body(): lax.ppermute(going_up, 'seq', [(d, (d + 1) % ways) for d in range(ways)])  9.17 us
  transfers between devices with their start and end apart: 19, of which 8 were waited for; matrix products, arithmetic and copies ran while one was open for 14% of the time, Pallas kernels for 0%

profile of v1, /device:TPU:1, one launch (start us, length us, event | category | flops | bytes accessed | tf_op | source)
XLA Modules:
  0.0 454.5 jit_solution(18057253395344388162)
XLA Ops:
  9.2 2.1 collective-permute-start
  12.1 1.3 slice_reduce_fusion
  13.4 2.0 fusion.126
  15.9 1.8 select_convert_fusion.2
  18.7 2.0 constant_dynamic-update-slice_fusion.15
  20.7 1.5 collective-permute-start.2
  23.2 2.9 fusion.123
  27.3 2.0 fusion.71
  30.1 4.2 select_reduce_fusion.1
  34.3 3.5 collective-permute-start.4
  39.7 5.9 %collective-permute-start.6 = (bf16[2,384,128]{2,1,0:T(8,128)(2,1)S(1)}, bf16[2,384,128]{2,1,0:T(8,128)(2,1)S(1)}, u32[]{:S(2)}, u32[]{:S(2)}) collective-permute-start(bf16[2,384,128]{2,1,0:T(8,128)(2,1)S(1)} %collective-permute-done.4), channel_id=1, source_target_pairs={{0,240},{16,0},{32,16},{48,32},{64,48},{80,64},{96,80},{112,96},{1... | collective-permute-start | bytes 589832 | tf_op jit(solution)/shard_map/ppermute | solution.py:126
  46.7 9.2 %collective-permute-start.8 = (bf16[2,384,128]{2,1,0:T(8,128)(2,1)S(1)}, bf16[2,384,128]{2,1,0:T(8,128)(2,1)S(1)}, u32[]{:S(2)}, u32[]{:S(2)}) collective-permute-start(bf16[2,384,128]{2,1,0:T(8,128)(2,1)S(1)} %collective-permute-done.6), channel_id=1, source_target_pairs={{0,240},{16,0},{32,16},{48,32},{64,48},{80,64},{96,80},{112,96},{1... | collective-permute-start | bytes 589832 | tf_op jit(solution)/shard_map/ppermute | solution.py:126
  57.0 9.6 %collective-permute-start.10 = (bf16[2,384,128]{2,1,0:T(8,128)(2,1)S(1)}, bf16[2,384,128]{2,1,0:T(8,128)(2,1)S(1)}, u32[]{:S(2)}, u32[]{:S(2)}) collective-permute-start(bf16[2,384,128]{2,1,0:T(8,128)(2,1)S(1)} %collective-permute-done.8), channel_id=1, source_target_pairs={{0,240},{16,0},{32,16},{48,32},{64,48},{80,64},{96,80},{112,96},{1... | collective-permute-start | bytes 589832 | tf_op jit(solution)/shard_map/ppermute | solution.py:126
  67.7 6.8 %collective-permute-start.12 = (bf16[2,384,128]{2,1,0:T(8,128)(2,1)S(1)}, bf16[2,384,128]{2,1,0:T(8,128)(2,1)S(1)}, u32[]{:S(2)}, u32[]{:S(2)}) collective-permute-start(bf16[2,384,128]{2,1,0:T(8,128)(2,1)S(1)} %collective-permute-done.10), channel_id=1, source_target_pairs={{0,240},{16,0},{32,16},{48,32},{64,48},{80,64},{96,80},{112,96},{1... | collective-permute-start | bytes 589832 | tf_op jit(solution)/shard_map/ppermute | solution.py:126
  75.5 5.2 %collective-permute-start.14 = (bf16[2,384,128]{2,1,0:T(8,128)(2,1)S(1)}, bf16[2,384,128]{2,1,0:T(8,128)(2,1)S(1)}, u32[]{:S(2)}, u32[]{:S(2)}) collective-permute-start(bf16[2,384,128]{2,1,0:T(8,128)(2,1)S(1)} %collective-permute-done.12), channel_id=1, source_target_pairs={{0,240},{16,0},{32,16},{48,32},{64,48},{80,64},{96,80},{112,96},{1... | collective-permute-start | bytes 589832 | tf_op jit(solution)/shard_map/ppermute | solution.py:126
  80.8 4.0 collective-permute-done.13
  86.0 5.2 %collective-permute-done.15 = bf16[2,384,128]{2,1,0:T(8,128)(2,1)S(1)} collective-permute-done((bf16[2,384,128]{2,1,0:T(8,128)(2,1)S(1)}, bf16[2,384,128]{2,1,0:T(8,128)(2,1)S(1)}, u32[]{:S(2)}, u32[]{:S(2)}) %collective-permute-start.15) | collective-permute-done | bytes 196640 | tf_op jit(solution)/shard_map/ppermute | solution.py:123
  93.1 44.4 %while.23 = (s32[]{:T(128)}, f32[8,192]{1,0:T(8,128)S(1)}, f32[8,192]{1,0:T(8,128)S(1)}, f32[8,192,128]{2,1,0:T(8,128)}, f32[8,192]{1,0:T(8,128)S(1)}, /*index=5...) while((s32[]{:T(128)}, f32[8,192]{1,0:T(8,128)S(1)}, ...), condition=%wide.region_15.16_spmd, body=%wide.region_6.15_spmd.sunk | while | flops 823598080 | bytes 43722840 | solution.py:166
  94.7 6.1 %conditional.4 = ((f32[8,192]{1,0:T(8,128)S(1)}, f32[8,192]{1,0:T(8,128)S(1)}, f32[8,192,128]{2,1,0:T(8,128)})) conditional(s32[]{:T(128)} %convert_element_type.400, (f32[8,192]{1,0:T(8,128)S(1)}, f32[8,192]{1,0:T(8,128)S(1)}, f32[8,192,128]{2,1,0:T(8,128)}) %tuple.75, (s32[]{:T(128)}, s32[192]{0:T(256)}, bf16[192,1024]{1,0:T(8,128)(2,1)}, ...), branch_computations={%region_7.7_spmd, %region_8.10_spmd} | conditional | flops 411799040 | bytes 18453340 | solution.py:157
  95.6 1.7 fusion
  98.5 1.5 fusion.14
  100.8 6.0 %conditional.5 = ((f32[8,192]{1,0:T(8,128)S(1)}, f32[8,192]{1,0:T(8,128)S(1)}, f32[8,192,128]{2,1,0:T(8,128)})) conditional(s32[]{:T(128)} %convert_element_type.401, (f32[8,192]{1,0:T(8,128)S(1)}, f32[8,192]{1,0:T(8,128)S(1)}, f32[8,192,128]{2,1,0:T(8,128)}) %tuple.77, (s32[]{:T(128)}, s32[192]{0:T(256)}, bf16[192,1024]{1,0:T(8,128)(2,1)}, ...), branch_computations={%region_11.11_spmd, %region_12.14_spmd} | conditional | flops 411799040 | bytes 18453340 | solution.py:157
  101.6 1.7 fusion.24
  104.5 1.5 fusion.38
  108.5 6.1 %conditional.4 = ((f32[8,192]{1,0:T(8,128)S(1)}, f32[8,192]{1,0:T(8,128)S(1)}, f32[8,192,128]{2,1,0:T(8,128)})) conditional(s32[]{:T(128)} %convert_element_type.400, (f32[8,192]{1,0:T(8,128)S(1)}, f32[8,192]{1,0:T(8,128)S(1)}, f32[8,192,128]{2,1,0:T(8,128)}) %tuple.75, (s32[]{:T(128)}, s32[192]{0:T(256)}, bf16[192,1024]{1,0:T(8,128)(2,1)}, ...), branch_computations={%region_7.7_spmd, %region_8.10_spmd} | conditional | flops 411799040 | bytes 18453340 | solution.py:157
  109.3 1.7 fusion
  112.2 1.5 fusion.14
  114.6 6.0 %conditional.5 = ((f32[8,192]{1,0:T(8,128)S(1)}, f32[8,192]{1,0:T(8,128)S(1)}, f32[8,192,128]{2,1,0:T(8,128)})) conditional(s32[]{:T(128)} %convert_element_type.401, (f32[8,192]{1,0:T(8,128)S(1)}, f32[8,192]{1,0:T(8,128)S(1)}, f32[8,192,128]{2,1,0:T(8,128)}) %tuple.77, (s32[]{:T(128)}, s32[192]{0:T(256)}, bf16[192,1024]{1,0:T(8,128)(2,1)}, ...), branch_computations={%region_11.11_spmd, %region_12.14_spmd} | conditional | flops 411799040 | bytes 18453340 | solution.py:157
  115.4 1.7 fusion.24
  118.3 1.5 fusion.38
  137.5 1.5 copy.125
  140.6 4.6 %slice.72 = bf16[16,8,128,128]{2,1,3,0:T(8,128)(2,1)} slice(bf16[16,8,128,129]{2,1,3,0:T(8,128)(2,1)} %all-gather.5.cloned.1.call-done), slice={[0:16], [0:8], [0:128], [0:128]} | slice | bytes 8388608 | tf_op jit(solution)/shard_map/slice | solution.py:26
  145.2 6.8 %copy.186 = bf16[16,8,128,128]{3,2,1,0:T(8,128)(2,1)} copy(bf16[16,8,128,128]{2,1,3,0:T(8,128)(2,1)} %slice.72) | data formatting | bytes 8388608
  152.0 3.3 select_reduce_fusion
  158.4 2.0 multiply_reduce_fusion
  162.5 2.8 fusion.128
  165.3 1.6 fusion.101
  166.9 1.9 add_select_fusion
  171.4 1.7 divide_multiply_fusion
  174.7 137.2 %all-gather.1 = bf16[128,128]{1,0:T(8,128)(2,1)S(1)} all-gather(bf16[8,128]{1,0:T(8,128)(2,1)S(1)} %add_convert_fusion), channel_id=3, replica_groups=mesh['seq'=16,'head'=16] {'seq'}, dimensions={0}, use_global_device_ids=true | all-gather | bytes 34816 | tf_op jit(solution)/shard_map/all_gather | solution.py:248
  312.0 4.7 %fusion.117 = f32[8,384,128]{2,1,0:T(8,128)S(1)} fusion(bf16[8,384,128]{2,1,0:T(8,128)(2,1)S(1)} %copy-done.3, f32[8,384,384]{1,2,0:T(8,128)} %copy-done.2), kind=kOutput, calls=%fused_computation.195 | convolution fusion | flops 306708480 | bytes 7077888 | tf_op jit(solution)/shard_map/hrs,hrf->hsf/dot_general | solution.py:49
  316.7 2.0 fusion.113
  318.7 6.4 %all-gather.7.cloned.1.call-done = bf16[128,128,128]{2,1,0:T(8,128)(2,1)} async-done(((bf16[8,128,128]{2,1,0:T(8,128)(2,1)}), bf16[128,128,128]{2,1,0:T(8,128)(2,1)}) %all-gather.7.cloned.1.call-update) | async-done | bytes 4194320 | tf_op jit(solution)/shard_map/all_gather | solution.py:245
  325.1 3.2 fusion.48
  329.8 2.6 fusion.55
  332.4 1.3 fusion.87
  333.7 1.3 fusion.72
  336.1 109.1 %all-reduce.2.cloned.1.call-done = bf16[262144]{0:T(1024)(128)(2,1)} async-done(((bf16[262144]{0:T(1024)(128)(2,1)}), bf16[262144]{0:T(1024)(128)(2,1)}) %all-reduce.2.cloned.1.call-update) | async-done | bytes 524304 | tf_op jit(solution)/shard_map/psum | solution.py:34
  (222 shorter events, 46.6 us)
Async XLA Ops:
  7.2 16.0 %copy-start = (bf16[8,128,128]{2,1,0:T(8,128)(2,1)S(1)}, bf16[8,128,128]{2,1,0:T(8,128)(2,1)}, u32[]{:S(2)}) copy-start(bf16[8,128,128]{2,1,0:T(8,128)(2,1)} %param.15) | copy-start | bytes 786436
  7.2 8.2 %copy-start.6 = (bf16[384,1024]{1,0:T(8,128)(2,1)S(1)}, bf16[384,1024]{1,0:T(8,128)(2,1)}, u32[]{:S(2)}) copy-start(bf16[384,1024]{1,0:T(8,128)(2,1)} %param.11) | copy-start | bytes 2359300
  7.2 8.2 %copy-start.21 = (bf16[8,128,128]{2,1,0:T(8,128)(2,1)S(1)}, bf16[8,128,128]{2,1,0:T(8,128)(2,1)}, u32[]{:S(2)}) copy-start(bf16[8,128,128]{2,1,0:T(8,128)(2,1)} %param.14) | copy-start | bytes 786436
  7.2 133.4 %all-gather.5.cloned.1.call-start = ((), (), s32[]{:S(2)}) async-start(), calls=%async_computation | async-start | bytes 4491264 | tf_op jit(solution)/shard_map/all_gather | solution.py:24
  9.2 6.6 %copy-start.15 = (bf16[384,64]{1,0:T(8,128)(2,1)}, bf16[384,64]{1,0:T(8,128)(2,1)S(1)}, u32[]{:S(2)}) copy-start(bf16[384,64]{1,0:T(8,128)(2,1)S(1)} %copy.116) | copy-start | bytes 147460
  9.2 9.0 %collective-permute-start = (bf16[2,384,64]{2,1,0:T(8,128)(2,1)S(1)}, bf16[2,384,64]{2,1,0:T(8,128)(2,1)}, u32[]{:S(2)}, u32[]{:S(2)}) collective-permute-start(bf16[2,384,64]{2,1,0:T(8,128)(2,1)S(1)} %pad_maximum_fusion.3), channel_id=1, source_target_pairs={{0,1},{1,0},{2,3},{3,2},{4,5},{5,4},{6,7},{7,6},{8,9},{9,8},{10,11... | collective-permute-start | bytes 294920 | tf_op jit(solution)/shard_map/ppermute | solution.py:18
  15.8 2.4 copy-start.4
  15.9 2.8 copy-start.16
  20.7 13.6 %collective-permute-start.2 = (bf16[2,384,128]{2,1,0:T(8,128)(2,1)}, bf16[2,384,128]{2,1,0:T(8,128)(2,1)}, u32[]{:S(2)}, u32[]{:S(2)}) collective-permute-start(bf16[2,384,128]{2,1,0:T(8,128)(2,1)} %get-tuple-element.353), channel_id=1, source_target_pairs={{0,240},{16,0},{32,16},{48,32},{64,48},{80,64},{96,80},{112,96},{1... | collective-permute-start | bytes 589832 | tf_op jit(solution)/shard_map/ppermute | solution.py:126
  22.2 15.6 %collective-permute-start.1 = (bf16[2,384,128]{2,1,0:T(8,128)(2,1)}, bf16[2,384,128]{2,1,0:T(8,128)(2,1)}, u32[]{:S(2)}, u32[]{:S(2)}) collective-permute-start(bf16[2,384,128]{2,1,0:T(8,128)(2,1)} %get-tuple-element.353), channel_id=1, source_target_pairs={{0,16},{16,32},{32,48},{48,64},{64,80},{80,96},{96,112},{112,128},... | collective-permute-start | bytes 589832 | tf_op jit(solution)/shard_map/ppermute | solution.py:123
  26.1 1.2 copy-start.14
  27.3 2.8 copy-start.17
  30.0 295.1 %all-gather.7.cloned.1.call-start = ((), (), s32[]{:S(2)}) async-start(), calls=%async_computation.2 | async-start | bytes 4456448 | tf_op jit(solution)/shard_map/all_gather | solution.py:245
  34.3 5.5 %collective-permute-start.4 = (bf16[2,384,128]{2,1,0:T(8,128)(2,1)}, bf16[2,384,128]{2,1,0:T(8,128)(2,1)S(1)}, u32[]{:S(2)}, u32[]{:S(2)}) collective-permute-start(bf16[2,384,128]{2,1,0:T(8,128)(2,1)} %collective-permute-done.2), channel_id=1, source_target_pairs={{0,240},{16,0},{32,16},{48,32},{64,48},{80,64},{96,80},{112,96},{1... | collective-permute-start | bytes 589832 | tf_op jit(solution)/shard_map/ppermute | solution.py:126
  37.8 7.9 %collective-permute-start.3 = (bf16[2,384,128]{2,1,0:T(8,128)(2,1)}, bf16[2,384,128]{2,1,0:T(8,128)(2,1)S(1)}, u32[]{:S(2)}, u32[]{:S(2)}) collective-permute-start(bf16[2,384,128]{2,1,0:T(8,128)(2,1)} %collective-permute-done.1), channel_id=1, source_target_pairs={{0,16},{16,32},{32,48},{48,64},{64,80},{80,96},{96,112},{112,128},... | collective-permute-start | bytes 589832 | tf_op jit(solution)/shard_map/ppermute | solution.py:123
  39.7 7.0 %collective-permute-start.6 = (bf16[2,384,128]{2,1,0:T(8,128)(2,1)S(1)}, bf16[2,384,128]{2,1,0:T(8,128)(2,1)S(1)}, u32[]{:S(2)}, u32[]{:S(2)}) collective-permute-start(bf16[2,384,128]{2,1,0:T(8,128)(2,1)S(1)} %collective-permute-done.4), channel_id=1, source_target_pairs={{0,240},{16,0},{32,16},{48,32},{64,48},{80,64},{96,80},{112,96},{1... | collective-permute-start | bytes 589832 | tf_op jit(solution)/shard_map/ppermute | solution.py:126
  45.7 10.3 %collective-permute-start.5 = (bf16[2,384,128]{2,1,0:T(8,128)(2,1)S(1)}, bf16[2,384,128]{2,1,0:T(8,128)(2,1)S(1)}, u32[]{:S(2)}, u32[]{:S(2)}) collective-permute-start(bf16[2,384,128]{2,1,0:T(8,128)(2,1)S(1)} %collective-permute-done.3), channel_id=1, source_target_pairs={{0,16},{16,32},{32,48},{48,64},{64,80},{80,96},{96,112},{112,128},... | collective-permute-start | bytes 589832 | tf_op jit(solution)/shard_map/ppermute | solution.py:123
  46.7 10.3 %collective-permute-start.8 = (bf16[2,384,128]{2,1,0:T(8,128)(2,1)S(1)}, bf16[2,384,128]{2,1,0:T(8,128)(2,1)S(1)}, u32[]{:S(2)}, u32[]{:S(2)}) collective-permute-start(bf16[2,384,128]{2,1,0:T(8,128)(2,1)S(1)} %collective-permute-done.6), channel_id=1, source_target_pairs={{0,240},{16,0},{32,16},{48,32},{64,48},{80,64},{96,80},{112,96},{1... | collective-permute-start | bytes 589832 | tf_op jit(solution)/shard_map/ppermute | solution.py:126
  56.0 10.6 %collective-permute-start.7 = (bf16[2,384,128]{2,1,0:T(8,128)(2,1)S(1)}, bf16[2,384,128]{2,1,0:T(8,128)(2,1)S(1)}, u32[]{:S(2)}, u32[]{:S(2)}) collective-permute-start(bf16[2,384,128]{2,1,0:T(8,128)(2,1)S(1)} %collective-permute-done.5), channel_id=1, source_target_pairs={{0,16},{16,32},{32,48},{48,64},{64,80},{80,96},{96,112},{112,128},... | collective-permute-start | bytes 589832 | tf_op jit(solution)/shard_map/ppermute | solution.py:123
  57.0 10.7 %collective-permute-start.10 = (bf16[2,384,128]{2,1,0:T(8,128)(2,1)S(1)}, bf16[2,384,128]{2,1,0:T(8,128)(2,1)S(1)}, u32[]{:S(2)}, u32[]{:S(2)}) collective-permute-start(bf16[2,384,128]{2,1,0:T(8,128)(2,1)S(1)} %collective-permute-done.8), channel_id=1, source_target_pairs={{0,240},{16,0},{32,16},{48,32},{64,48},{80,64},{96,80},{112,96},{1... | collective-permute-start | bytes 589832 | tf_op jit(solution)/shard_map/ppermute | solution.py:126
  66.6 7.8 %collective-permute-start.9 = (bf16[2,384,128]{2,1,0:T(8,128)(2,1)S(1)}, bf16[2,384,128]{2,1,0:T(8,128)(2,1)S(1)}, u32[]{:S(2)}, u32[]{:S(2)}) collective-permute-start(bf16[2,384,128]{2,1,0:T(8,128)(2,1)S(1)} %collective-permute-done.7), channel_id=1, source_target_pairs={{0,16},{16,32},{32,48},{48,64},{64,80},{80,96},{96,112},{112,128},... | collective-permute-start | bytes 589832 | tf_op jit(solution)/shard_map/ppermute | solution.py:123
  67.7 7.8 %collective-permute-start.12 = (bf16[2,384,128]{2,1,0:T(8,128)(2,1)S(1)}, bf16[2,384,128]{2,1,0:T(8,128)(2,1)S(1)}, u32[]{:S(2)}, u32[]{:S(2)}) collective-permute-start(bf16[2,384,128]{2,1,0:T(8,128)(2,1)S(1)} %collective-permute-done.10), channel_id=1, source_target_pairs={{0,240},{16,0},{32,16},{48,32},{64,48},{80,64},{96,80},{112,96},{1... | collective-permute-start | bytes 589832 | tf_op jit(solution)/shard_map/ppermute | solution.py:126
  74.5 6.3 %collective-permute-start.11 = (bf16[2,384,128]{2,1,0:T(8,128)(2,1)S(1)}, bf16[2,384,128]{2,1,0:T(8,128)(2,1)S(1)}, u32[]{:S(2)}, u32[]{:S(2)}) collective-permute-start(bf16[2,384,128]{2,1,0:T(8,128)(2,1)S(1)} %collective-permute-done.9), channel_id=1, source_target_pairs={{0,16},{16,32},{32,48},{48,64},{64,80},{80,96},{96,112},{112,128},... | collective-permute-start | bytes 589832 | tf_op jit(solution)/shard_map/ppermute | solution.py:123
  75.5 10.4 %collective-permute-start.14 = (bf16[2,384,128]{2,1,0:T(8,128)(2,1)S(1)}, bf16[2,384,128]{2,1,0:T(8,128)(2,1)S(1)}, u32[]{:S(2)}, u32[]{:S(2)}) collective-permute-start(bf16[2,384,128]{2,1,0:T(8,128)(2,1)S(1)} %collective-permute-done.12), channel_id=1, source_target_pairs={{0,240},{16,0},{32,16},{48,32},{64,48},{80,64},{96,80},{112,96},{1... | collective-permute-start | bytes 589832 | tf_op jit(solution)/shard_map/ppermute | solution.py:126
  80.8 4.1 collective-permute-start.13
  84.8 6.3 %collective-permute-start.15 = (bf16[2,384,128]{2,1,0:T(8,128)(2,1)S(1)}, bf16[2,384,128]{2,1,0:T(8,128)(2,1)S(1)}, u32[]{:S(2)}, u32[]{:S(2)}) collective-permute-start(bf16[2,384,128]{2,1,0:T(8,128)(2,1)S(1)} %collective-permute-done.13), channel_id=1, source_target_pairs={{0,16},{16,32},{32,48},{48,64},{64,80},{80,96},{96,112},{112,128},... | collective-permute-start | bytes 589832 | tf_op jit(solution)/shard_map/ppermute | solution.py:123
  97.3 1.1 copy-start.11
  103.3 1.1 copy-start.9
  106.0 0.9 copy-start.10
  111.1 1.1 copy-start.11
  117.1 1.1 copy-start.9
  119.8 0.9 copy-start.10
  137.5 1.6 copy-start.13
  145.2 6.8 %copy-start.23 = (pred[16]{0:T(512)(128)(4,1)S(1)}, pred[16]{0:T(512)(128)(4,1)}, u32[]{:S(2)}) copy-start(pred[16]{0:T(512)(128)(4,1)} %iota_compare_fusion.2) | copy-start | bytes 52
  152.0 3.5 copy-start.3
  156.0 2.4 copy-start.22
  156.0 2.4 copy-start.18
  156.0 2.4 copy-start.19
  156.0 2.4 copy-start.20
  156.0 2.4 copy-start.24
  162.2 283.0 %all-reduce.2.cloned.1.call-start = ((), (), s32[]{:S(2)}) async-start(), calls=%async_computation.1 | async-start | bytes 1048576 | tf_op jit(solution)/shard_map/psum | solution.py:34
  166.9 1.9 copy-start.8
  168.8 2.1 copy-start.2
  168.9 2.6 copy-start.5
  171.4 1.7 copy-start.7
  173.1 143.6 %slice-start = ((s8[4718592]{0:T(1024)(128)(4,1)}), s8[524288]{0:T(1024)(128)(4,1)S(1)}, s32[]{:S(2)}) async-start(s8[4718592]{0:T(1024)(128)(4,1)} %bitcast.271), calls=%async_computation.3 | async-start | bytes 1048576
  174.5 142.3 %slice-start.1 = ((s8[4718592]{0:T(1024)(128)(4,1)}), s8[4194304]{0:T(1024)(128)(4,1)S(1)}, s32[]{:S(2)}) async-start(s8[4718592]{0:T(1024)(128)(4,1)} %bitcast.271), calls=%async_computation.4 | async-start | bytes 8388608
  333.7 114.2 %copy-start.1 = (bf16[8,128,128]{2,1,0:T(8,128)(2,1)S(1)}, bf16[8,128,128]{2,1,0:T(8,128)(2,1)}, u32[]{:S(2)}) copy-start(bf16[8,128,128]{2,1,0:T(8,128)(2,1)} %param.15) | copy-start | bytes 786436
  (2 other events, 1.8 us)
Sparse Core Ops, SparseCore 0:
  30.2 46.8 all-gather.4
  162.3 162.7 all-gather.6
  336.2 108.9 all-reduce.1
